TPU v7x, 256 devices: a whole 4x4x8 slice. The times are simulated.
256 devices in a mesh: snap: 16 (over z, x_hi), mesh: 16 (over x_lo, y, core).
Axes of the slice: x: 4 (x_hi: 2, x_lo: 2; x = x_hi * 2 + x_lo), y: 4, z: 8, core: 2. Of those that a mesh axis runs over, the one named last changes fastest.
Arguments:
- snapshots: float32 [49152, 2048], P('mesh', 'snap'), may hold values from -6 to 6
- region_ids: int32 [96, 512], P('mesh'), may hold values from 0 to 7
- conductivity: float32 [8], replicated, may hold values from 0.2 to 5
Outputs:
- gram: float32 [2048, 2048], P('snap', 'mesh')
All inputs are finite; a program needn't handle non-finite values.
Results may differ from a plain program's by a relative error of at most 0.0003.
Values sent between devices are 32-bit elements; how exact they have to be, the bound alone decides.
A program may use at most 128 MiB of HBM per device.

v0:
```python
import math
import jax
import jax.numpy as jnp
from jax import lax
from jax.sharding import PartitionSpec as P


def passed_along(value, axis, steps):
    count = lax.axis_size(axis)
    first, last = (max(0, -steps), min(count, count - steps))
    return lax.ppermute(value, axis, [(source, source + steps) for source in range(first, last)])


def weights_of(region_ids, conductivity):
    table = jnp.arange(conductivity.shape[0], dtype=jnp.int32)
    picked = jnp.where(
        region_ids[:, :, None] == table[None, None, :],
        conductivity[None, None, :],
        jnp.zeros((), conductivity.dtype),
    )
    return jnp.sum(picked, axis=-1) / 36.0


def element_terms(field, below, weight):
    lower = jnp.concatenate([field, below[None]], 0)
    padded = jnp.pad(lower, ((0, 0), (0, 1), (0, 0)))
    corner_a = padded[:-1, :-1]
    corner_b = padded[:-1, 1:]
    corner_e = padded[1:, :-1]
    corner_d = padded[1:, 1:]
    scaled = weight[:, :, None]
    to_a = scaled * (4.0 * corner_a + 2.0 * corner_b + 2.0 * corner_e + corner_d)
    to_b = scaled * (2.0 * corner_a + 4.0 * corner_b + corner_e + 2.0 * corner_d)
    to_e = scaled * (2.0 * corner_a + corner_b + 4.0 * corner_e + 2.0 * corner_d)
    to_d = scaled * (corner_a + 2.0 * corner_b + 2.0 * corner_e + 4.0 * corner_d)
    total = jnp.pad(to_a, ((0, 1), (0, 1), (0, 0))) + jnp.pad(to_b, ((0, 1), (1, 0), (0, 0)))
    total = (
        total + jnp.pad(to_e, ((1, 0), (0, 1), (0, 0))) + jnp.pad(to_d, ((1, 0), (1, 0), (0, 0)))
    )
    return total


def contract(left, right):
    return lax.dot_general(
        left,
        right,
        (((0,), (0,)), ((), ())),
        precision=lax.Precision.HIGHEST,
        preferred_element_type=jnp.float32,
    )


def local(snapshots, region_ids, conductivity):
    strip, width = region_ids.shape
    node_rows, group_cols = snapshots.shape
    field = snapshots.reshape(strip, width, group_cols)
    weight = weights_of(region_ids, conductivity)
    below = passed_along(field[0], "mesh", -1)
    total = element_terms(field, below, weight)
    carried = passed_along(total[strip, :width], "mesh", 1)
    inner = total[:strip, :width]
    panel = jnp.concatenate([inner[:1] + carried[None], inner[1:]], 0).reshape(
        node_rows, group_cols
    )
    partial_value = contract(snapshots, lax.all_gather(panel, "snap", axis=1, tiled=True))
    summed = lax.psum_scatter(partial_value, "mesh", scatter_dimension=1, tiled=True)
    total_nodes = node_rows * lax.axis_size("mesh")
    return summed / math.sqrt(total_nodes)


def solution(mesh):
    return jax.shard_map(
        local,
        mesh=mesh,
        in_specs=(P("mesh", "snap"), P("mesh", None), P()),
        out_specs=P("snap", "mesh"),
        check_vma=False,
    )
```

profile of v0, /device:TPU:32, one launch (start us, length us, event | category | flops | bytes accessed | tf_op | source)
XLA Modules:
  0.0 477.0 jit_solution(9330290577570268332)
XLA Ops:
  6.5 0.0 all-gather.2.cloned.1.call-start
  6.5 1.0 slice.28
  7.5 1.3 collective-permute-start
  8.8 0.8 select_reduce_fusion
  9.7 1.3 collective-permute-done
  10.9 0.0 copy-start
  10.9 1.6 pad_maximum_fusion
  12.6 0.2 copy-done
  12.8 0.6 add_multiply_fusion.3
  13.5 1.3 add_multiply_fusion.2
  14.8 6.1 %collective-permute-start.1 = (f32[512,128]{1,0:T(8,128)S(1)}, f32[512,128]{1,0:T(8,128)S(1)}, u32[]{:S(2)}, u32[]{:S(2)}) collective-permute-start(f32[512,128]{1,0:T(8,128)S(1)} %add_bitcast_fusion), channel_id=1, source_target_pairs={{0,1},{1,2},{2,3},{3,4},{4,5},{5,6},{6,7},{7,8},{8,9},{9,10},{10,1... | collective-permute-start | bytes 786440 | tf_op jit(solution)/shard_map/ppermute | solution.py:11
  20.9 0.3 pad_add_fusion
  21.2 0.8 collective-permute-done.1
  22.0 0.1 add_add_fusion
  22.1 1.3 pad_maximum_fusion.1
  23.4 0.0 all-gather.2.cloned.1.call-update
  23.5 0.0 reduce-scatter.2.cloned.1.call-start
  23.5 340.8 %all-gather.2.cloned.1.call-done = f32[3072,2048]{1,0:T(8,128)} async-done(((f32[3072,128]{1,0:T(8,128)}), f32[3072,2048]{1,0:T(8,128)}) %all-gather.2.cloned.1.call-update) | async-done | bytes 25165840 | tf_op jit(solution)/shard_map/all_gather | solution.py:65
  364.4 43.1 %convolution_bitcast_fusion = f32[128,2048]{0,1:T(8,128)} fusion(f32[3072,2048]{1,0:T(8,128)} %all-gather.2.cloned.1.call-done, f32[3072,128]{1,0:T(8,128)S(1)} %copy-done), kind=kOutput, calls=%fused_computation.2 | convolution fusion | flops 9663676416 | bytes 27787264 | tf_op jit(solution)/shard_map/dot_general | solution.py:44
  407.5 0.0 reduce-scatter.2.cloned.1.call-update
  407.5 61.1 %reduce-scatter.2.cloned.1.call-done = f32[128,128]{0,1:T(8,128)} async-done(((f32[128,2048]{0,1:T(8,128)}), f32[128,128]{0,1:T(8,128)}) %reduce-scatter.2.cloned.1.call-update) | async-done | bytes 65552 | tf_op jit(solution)/shard_map/reduce_scatter | solution.py:66
  468.6 0.8 broadcast_multiply_fusion
  469.4 0.7 copy.5
  (2 shorter events, 0.0 us)
Async XLA Ops:
  6.5 357.8 %all-gather.2.cloned.1.call-start = ((), (), s32[]{:S(2)}) async-start(), calls=%async_computation.1 | async-start | bytes 26738688 | tf_op jit(solution)/shard_map/all_gather | solution.py:65
  7.5 3.4 collective-permute-start
  10.9 1.9 copy-start
  14.8 7.3 %collective-permute-start.1 = (f32[512,128]{1,0:T(8,128)S(1)}, f32[512,128]{1,0:T(8,128)S(1)}, u32[]{:S(2)}, u32[]{:S(2)}) collective-permute-start(f32[512,128]{1,0:T(8,128)S(1)} %add_bitcast_fusion), channel_id=1, source_target_pairs={{0,1},{1,2},{2,3},{3,4},{4,5},{5,6},{6,7},{7,8},{8,9},{9,10},{10,1... | collective-permute-start | bytes 786440 | tf_op jit(solution)/shard_map/ppermute | solution.py:11
  23.5 445.1 %reduce-scatter.2.cloned.1.call-start = ((), (), s32[]{:S(2)}) async-start(), calls=%async_computation.2 | async-start | bytes 1114112 | tf_op jit(solution)/shard_map/reduce_scatter | solution.py:66
Sparse Core Ops, SparseCore 0:
  23.6 340.7 all-gather.1
  407.6 60.8 reduce-scatter.1
where the time goes:
time: 477 us
  waiting for transfers between devices  404 us (85%)
  matrix products  43.1 us (9%)
  between operations  13.5 us (3%)
  starting transfers between devices  7.48 us (2%)
  other arithmetic  6.95 us (1%)
    all_gather x1, waiting for transfers between devices, local(): lax.all_gather(panel, 'snap', axis=1, tiled=True)  341 us
    reduce_scatter x1, waiting for transfers between devices, local(): lax.psum_scatter(partial_value, 'mesh', scatter_dimension=1, tiled=True)  61.1 us
    dot_general x1, matrix products, contract(): lax.dot_general(left, right, (((0,), (0,)), ((), ())), precision=lax.Prec...  43.1 us
  transfers between devices with their start and end apart: 4, of which 4 were waited for; matrix products, arithmetic and copies ran while one was open for 0% of the time, Pallas kernels for 0%

commit v1 on v0

--- a/solution.py
+++ b/solution.py
@@ -62,7 +62,12 @@
     panel = jnp.concatenate([inner[:1] + carried[None], inner[1:]], 0).reshape(
         node_rows, group_cols
     )
-    partial_value = contract(snapshots, lax.all_gather(panel, "snap", axis=1, tiled=True))
+    partial_value = contract(
+        snapshots,
+        jnp.concatenate(
+            lax.all_to_all(jnp.stack([panel] * lax.axis_size("snap")), "snap", 0, 0), axis=1
+        ),
+    )
     summed = lax.psum_scatter(partial_value, "mesh", scatter_dimension=1, tiled=True)
     total_nodes = node_rows * lax.axis_size("mesh")
     return summed / math.sqrt(total_nodes)

time: 477 us -> 687 us (1.44)
  blocking collectives: 0 us -> 556 us
  waiting for transfers between devices: 404 us -> 66.8 us
  matrix products: 43.1 us -> 20.9 us
  local copies, waits for them, and re-layouts: 1.92 us -> 16.5 us
    all_to_all x0 -> x1, blocking collectives: none -> 556 us  [local(): lax.all_to_all(jnp.stack([panel] * lax.axis_size('snap')), 'snap', 0, 0)]
    all_gather x1 -> x0, waiting for transfers between devices: 341 us -> none  [local(): lax.all_gather(panel, 'snap', axis=1, tiled=True)]
    dot_general x1, matrix products: 43.1 us -> 20.9 us  [contract(): lax.dot_general(left, right, (((0,), (0,)), ((), ())), precision=lax.Prec...]
    another operation x0 -> x2, local copies, waits for them, and re-layouts: none -> 14.6 us  [local(): jnp.stack([panel] * lax.axis_size('snap'))]
  transfers between devices with their start and end apart: 4 -> 3, of which waited for: 4 -> 3; matrix products, arithmetic and copies ran while one was open for 0% -> 0% of each run, Pallas kernels for 0% -> 0%
where the time goes in v1:
time: 687 us
  blocking collectives  556 us (81%)
  waiting for transfers between devices  66.8 us (10%)
  matrix products  20.9 us (3%)
  local copies, waits for them, and re-layouts  16.5 us (2%)
  between operations  13.5 us (2%)
  starting transfers between devices  7.43 us (1%)
    all_to_all x1, blocking collectives, local(): lax.all_to_all(jnp.stack([panel] * lax.axis_size('snap')), 'snap', 0, 0)  556 us
    reduce_scatter x1, waiting for transfers between devices, local(): lax.psum_scatter(partial_value, 'mesh', scatter_dimension=1, tiled=True)  64.7 us
    dot_general x1, matrix products, contract(): lax.dot_general(left, right, (((0,), (0,)), ((), ())), precision=lax.Prec...  20.9 us
    another operation x2, local copies, waits for them, and re-layouts, local(): jnp.stack([panel] * lax.axis_size('snap'))  14.6 us
  transfers between devices with their start and end apart: 3, of which 3 were waited for; matrix products, arithmetic and copies ran while one was open for 0% of the time, Pallas kernels for 0%

profile of v1, /device:TPU:32, one launch (start us, length us, event | category | flops | bytes accessed | tf_op | source)
XLA Modules:
  0.0 687.1 jit_solution(6887407007268764826)
XLA Ops:
  6.5 0.0 reduce-scatter.2.cloned.1.call-start
  6.5 1.0 slice.28
  7.5 1.3 collective-permute-start
  8.8 0.8 select_reduce_fusion
  9.7 1.3 collective-permute-done
  10.9 0.0 copy-start
  10.9 1.6 pad_maximum_fusion
  12.6 0.2 copy-done
  12.8 0.6 add_multiply_fusion.3
  13.5 1.3 add_multiply_fusion.2
  14.8 6.1 collective-permute-start.1
  20.9 0.3 pad_add_fusion
  21.2 0.8 collective-permute-done.1
  22.0 0.1 add_add_fusion
  22.1 0.1 pad_maximum_fusion.1
  22.2 1.7 copy.9
  23.9 12.9 %stack.3 = f32[16,3072,128]{1,2,0:T(8,128)} broadcast(f32[3072,128]{0,1:T(8,128)} %copy.9), dimensions={1,2} | broadcast | bytes 26738688 | tf_op jit(solution)/shard_map/stack | solution.py:68
  36.8 556.2 %all_to_all.5 = f32[16,3072,128]{1,2,0:T(8,128)S(1)} all-to-all(f32[16,3072,128]{1,2,0:T(8,128)} %stack.3), channel_id=1, replica_groups=mesh['snap'=16,'mesh'=16] {'snap'}, dimensions={0} | all-to-all | bytes 50331648 | tf_op jit(solution)/shard_map/all_to_all | solution.py:68
  593.1 20.9 %convolution_bitcast_fusion = f32[128,2048]{0,1:T(8,128)} fusion(f32[3072,2048]{0,1:T(8,128)S(1)} %bitcast.14, f32[3072,128]{1,0:T(8,128)S(1)} %copy-done), kind=kOutput, calls=%fused_computation.2 | convolution fusion | flops 9663676416 | bytes 27787264 | tf_op jit(solution)/shard_map/dot_general | solution.py:44
  614.0 0.0 reduce-scatter.2.cloned.1.call-update
  614.0 64.7 %reduce-scatter.2.cloned.1.call-done = f32[128,128]{0,1:T(8,128)} async-done(((f32[128,2048]{0,1:T(8,128)}), f32[128,128]{0,1:T(8,128)}) %reduce-scatter.2.cloned.1.call-update) | async-done | bytes 65552 | tf_op jit(solution)/shard_map/reduce_scatter | solution.py:71
  678.7 0.8 broadcast_multiply_fusion
  679.5 0.7 copy.10
  (2 shorter events, 0.0 us)
Async XLA Ops:
  6.5 672.1 %reduce-scatter.2.cloned.1.call-start = ((), (), s32[]{:S(2)}) async-start(), calls=%async_computation.2 | async-start | bytes 1114112 | tf_op jit(solution)/shard_map/reduce_scatter | solution.py:71
  7.5 3.4 collective-permute-start
  10.9 1.9 copy-start
  14.8 7.3 %collective-permute-start.1 = (f32[512,128]{1,0:T(8,128)S(1)}, f32[512,128]{1,0:T(8,128)S(1)}, u32[]{:S(2)}, u32[]{:S(2)}) collective-permute-start(f32[512,128]{1,0:T(8,128)S(1)} %add_bitcast_fusion), channel_id=1, source_target_pairs={{0,1},{1,2},{2,3},{3,4},{4,5},{5,6},{6,7},{7,8},{8,9},{9,10},{10,1... | collective-permute-start | bytes 786440 | tf_op jit(solution)/shard_map/ppermute | solution.py:11
Sparse Core Ops, SparseCore 0:
  614.1 64.4 reduce-scatter.1
